TPU v7x, 32 devices: a whole 2x2x4 slice. The times are simulated.
32 devices in a mesh: gx: 8 (over y, x, core), gy: 4 (over z).
Axes of the slice: x: 2, y: 2, z: 4, core: 2. Of those that a mesh axis runs over, the one named last changes fastest.
Arguments:
- velocity: float32 [3, 32, 256, 2048], P(None, None, 'gx', 'gy'), may hold values from -6 to 6
- fiber_points: float32 [256, 3, 128], P(('gx', 'gy')), may hold values from -6 to 6
- stiffness: float32 [256], P(('gx', 'gy')), may hold values from 0.5 to 2
- links: int32 [256, 128], P(('gx', 'gy')), may hold values from 1 to 127
- delta_weights: bfloat16 [256, 8, 128, 512], P(('gx', 'gy')), may hold values from -0.5 to 0.5
- owners: int32 [256, 8, 1], P(('gx', 'gy')), may hold values from 0 to 31; in each aligned block of 64 rows (0 to 63, 64 to 127, ..., all dimensions but the last counted through in order) at most 4 rows name the same one
- patch_slots: int32 [256, 8], P(('gx', 'gy')), may hold values from 0 to 1023
Outputs:
- fluid: float32 [3, 32, 256, 2048], P(None, None, 'gx', 'gy')
- moved_points: float32 [256, 3, 128], P(('gx', 'gy'))
Inputs may be any that keep to these rules, and one draw needn't show every extreme that they name: owners counts devices in the order gx slower, gy faster; among the rows of one device, no owner is named more than 4 times, a bound that some block reaches.
All inputs are finite; a program needn't handle non-finite values.
Results may differ from a plain program's by a relative error of at most 0.0037.
Values may be sent and summed in bfloat16 or wider, within the bound.
A program may use at most 128 MiB of HBM per device.

v0:
```python
import functools

import jax
import jax.numpy as jnp
from jax import lax
from jax.experimental import pallas as pl
from jax.experimental.pallas import tpu as pltpu
from jax.sharding import PartitionSpec as P

STEPS = 2
viscosity = 0.1
transport_rate = 0.1
force_step = 0.5
fiber_step = 0.25

F32 = jnp.float32
BF16 = jnp.bfloat16
I32 = jnp.int32
LANES = 128
MESH = pl.DeviceIdType.MESH
VMEM = pl.BlockSpec(memory_space=pltpu.VMEM)
ANY = pl.BlockSpec(memory_space=pl.ANY)
SMEM = pl.BlockSpec(memory_space=pltpu.SMEM)


def iota(shape, dim):
    return lax.broadcasted_iota(I32, shape, dim)


def to_column(row):
    n = row.shape[1]
    return jnp.sum(jnp.where(iota((n, n), 0) == iota((n, n), 1), row, 0), axis=1, keepdims=True)


def to_row(grid):
    n, k = grid.shape
    tiled = jnp.concatenate([grid] * n, axis=1)
    return jnp.sum(
        jnp.where(iota((n, n * k), 0) == iota((n, n * k), 1) // k, tiled, 0), axis=0, keepdims=True)


def slot_row(owner_row, owner_column, devices):
    n = owner_row.shape[1]
    same = (owner_column == owner_row) & (iota((n, n), 0) < iota((n, n), 1))
    rank = jnp.sum(jnp.where(same, 1, 0), axis=0, keepdims=True)
    return rank * devices + owner_row


def slot_column(owner_row, owner_column, devices):
    n = owner_row.shape[1]
    same = (owner_column == owner_row) & (iota((n, n), 1) < iota((n, n), 0))
    rank = jnp.sum(jnp.where(same, 1, 0), axis=1, keepdims=True)
    return rank * devices + owner_column


def spread(
    devices, per_owner, points_ref, stiffness_ref, links_ref, owners_ref, slots_ref, loaded_ref,
    out_ref, table_ref, contrib_ref, stage_ref, wait_block,
):
    blocks, k, points, patch = loaded_ref.shape
    parts = []
    for c in range(3):
        rest = points_ref[c]
        for _ in range(3):
            part = rest.astype(BF16).astype(F32)
            parts.append(part)
            rest = rest - part
    parts.append(jnp.zeros_like(parts[0]))
    parts = jnp.concatenate(parts, axis=0).astype(BF16)
    partner = lax.rem(iota(links_ref.shape, 1) + links_ref[...], points)
    diagonal = iota((k, k * points), 0) == iota((k, k * points), 1) // points
    lefts = []
    for b in range(blocks):
        moving = one_hot(iota((points, points), 0) == partner[b:b + 1])
        there = jnp.dot(parts, moving, preferred_element_type=F32)
        rows = []
        for c in range(3):
            r = 3 * c * blocks + b
            found = there[r:r + 1] + there[r + blocks:r + blocks + 1]
            found = found + there[r + 2 * blocks:r + 2 * blocks + 1]
            row = stiffness_ref[b] * (found - points_ref[c, b:b + 1, :])
            rows.append(jnp.where(diagonal, jnp.concatenate([row] * k, axis=1), 0.0))
        rows.append(jnp.zeros_like(rows[0]))
        lefts.append(jnp.concatenate(rows, axis=0).astype(BF16))

    owner_row = to_row(owners_ref[:, 0, :])
    places = slot_row(owner_row, to_column(owner_row), devices)
    total = devices * per_owner
    chosen = iota((total, places.shape[1]), 0) == places
    selector = one_hot(chosen)

    for b in range(blocks):
        wait_block(b)
        right = loaded_ref[b].reshape(k * points, patch)
        result = jnp.dot(lefts[b], right, preferred_element_type=F32)
        for c in range(3):
            contrib_ref[c, b * k:(b + 1) * k, :] = result[c * k:(c + 1) * k]

    tiles = patch // LANES
    width = 3 * tiles * per_owner
    for c in range(3):
        packed = jnp.dot(selector, contrib_ref[c].astype(BF16), preferred_element_type=F32)
        for p in range(per_owner):
            for t in range(tiles):
                stage_ref[pl.ds(p * 3 * tiles + c * tiles + t, devices, stride=width), :] = (
                    packed[p * devices:(p + 1) * devices, t * LANES:(t + 1) * LANES]
                )
    out_ref[...] = stage_ref[...].reshape(out_ref.shape).astype(BF16)
    column = jnp.max(jnp.where(chosen, to_row(slots_ref[...]), -1), axis=1, keepdims=True)
    lane = iota((devices, LANES), 1)
    table = jnp.full((devices, LANES), -1, I32)
    for p in range(per_owner):
        table = jnp.where(lane == p, column[p * devices:(p + 1) * devices], table)
    for d in range(devices):
        table_ref[d] = table[d:d + 1]


HBM = pl.BlockSpec(memory_space=pltpu.HBM)


def place(d, columns):
    return (d // columns, lax.rem(d, columns))


def start_swap(columns, devices, ins, outs, send_sem, recv_sem, own_sem):
    count = len(ins)
    me = lax.axis_index("gx") * columns + lax.axis_index("gy")

    def copy(n, off):
        other = lax.rem(me + off, devices)
        return pltpu.make_async_remote_copy(
            src_ref=ins[n].at[other], dst_ref=outs[n].at[me],
            send_sem=send_sem.at[n, off], recv_sem=recv_sem.at[n, off],
            device_id=place(other, columns), device_id_type=MESH,
        )

    def start(off, carry):
        for n in range(count):
            copy(n, off).start()
        return carry

    def finish(off, carry):
        for n in range(count):
            copy(n, off).wait()
        return carry

    def own(n):
        return pltpu.make_async_copy(ins[n].at[me], outs[n].at[me], own_sem.at[n])

    lax.fori_loop(1, devices, start, 0)
    for n in range(count):
        own(n).start()

    def wait():
        for n in range(count):
            own(n).wait()
        lax.fori_loop(1, devices, finish, 0)

    return wait


def swap_sems(count, devices):
    return [
        pltpu.SemaphoreType.DMA((count, devices)),
        pltpu.SemaphoreType.DMA((count, devices)),
        pltpu.SemaphoreType.DMA((count,)),
    ]


def unpack(stage_ref, devices, per_owner, tiles, c):
    width = 3 * tiles * per_owner
    rows = []
    for p in range(per_owner):
        rows.append(jnp.concatenate(
            [stage_ref[pl.ds(p * 3 * tiles + c * tiles + t, devices, stride=width), :]
             for t in range(tiles)], axis=1))
    return jnp.concatenate(rows, axis=0)


def table_row(table_ref, devices, per_owner):
    total = devices * per_owner
    row = jnp.zeros((1, total), I32)
    for p in range(per_owner):
        column = table_ref[:, 0, :][:, p:p + 1]
        spot = iota((devices, total), 1) == p * devices + iota((devices, total), 0)
        row = row + jnp.sum(jnp.where(spot, column, 0), axis=0, keepdims=True)
    return row


def table_column(table_ref, per_owner):
    return jnp.concatenate([table_ref[:, 0, :][:, p:p + 1] for p in range(per_owner)], axis=0)


def one_hot(mask):
    return mask.astype(F32).astype(BF16)


PAD = 8
UNROLL = 4
assert viscosity == transport_rate
keep = 1.0 - 6.0 * viscosity


def sweep(mid, east, west, north, south, above, below):
    coefficients = [(1 - m, 1 + m) for m in mid]
    out = []
    for c in range(3):
        pairs = [
            ahead * front[c] + behind * back[c]
            for (ahead, behind), (front, back) in zip(
                coefficients, ((east, west), (north, south), (above, below)))
        ]
        out.append(pairs[0] + (pairs[1] + pairs[2]))
    return out


def step_kernel(
    rows_grid, columns_grid, per_owner, unroll, points_in, stiffness_in, links_in, owners_in,
    slots_in, weights_ref, velocity_ref,
    fluid_ref, interp_ref, loaded_ref, returned_ref, picked_ref,
    points_ref, stiffness_ref, links_ref, owners_ref, slots_ref, small_sem, received_ref, table_ref, out_ref, outtable_ref, replies_ref, contrib_ref, stage_ref,
    force_ref, first_ref, second_ref, first_half, second_half, taking_ref, sides_send, sides_recv, ends_send, ends_recv,
    halo_ref, send_sem, recv_sem, own_sem, rsend_sem, rrecv_sem, rown_sem, load_sem, block_sem,
    hsend_sem, hrecv_sem,
):
    devices = rows_grid * columns_grid
    total = devices * per_owner
    tiles, _, layers, rows, _ = fluid_ref.shape
    blocks = weights_ref.shape[0]
    groups = rows // 8
    order = [*range(1, groups - 1), groups - 1, 0]
    pairs = [tuple(order[n:n + 2]) for n in range(0, groups, 2)]
    stride = first_ref.shape[3]
    flat_shape = (3, tiles, layers * stride, LANES)

    def block(b):
        return pltpu.make_async_copy(weights_ref.at[b], loaded_ref.at[b], block_sem.at[b])

    def load(t):
        return pltpu.make_async_copy(
            velocity_ref.at[:, :, :, pl.ds(t * LANES, LANES)], fluid_ref.at[t], load_sem.at[t])

    small = [
        pltpu.make_async_copy(source, target, small_sem.at[n])
        for n, (source, target) in enumerate((
            (points_in, points_ref), (stiffness_in, stiffness_ref), (links_in, links_ref),
            (owners_in, owners_ref), (slots_in, slots_ref)))
    ]
    for copy in small:
        copy.start()
    for b in range(blocks):
        block(b).start()
    for t in range(tiles):
        load(t).start()

    gx, gy = lax.axis_index("gx"), lax.axis_index("gy")
    me = gx * columns_grid + gy
    barrier = pltpu.get_barrier_semaphore()

    def hello(off, carry):
        other = lax.rem(me + off, devices)
        pl.semaphore_signal(
            barrier, inc=1, device_id=place(other, columns_grid), device_id_type=MESH)
        return carry

    lax.fori_loop(1, devices, hello, 0)
    for copy in small:
        copy.wait()
    spread(
        devices, per_owner, points_ref, stiffness_ref, links_ref, owners_ref, slots_ref,
        loaded_ref, out_ref, outtable_ref, contrib_ref, stage_ref, lambda b: block(b).wait())
    pl.semaphore_wait(barrier, devices - 1)
    wait = start_swap(
        columns_grid, devices, [out_ref, outtable_ref], [received_ref, table_ref],
        send_sem, recv_sem, own_sem)
    for t in range(tiles):
        load(t).wait()
    wait()

    stage_ref[...] = received_ref[...].astype(F32).reshape(stage_ref.shape)
    for c in range(3):
        force_ref[c] = (force_step * unpack(stage_ref, devices, per_owner, tiles, c)).astype(BF16)
    slots_row = table_row(table_ref, devices, per_owner)
    chunk = 8
    cells = chunk * rows
    lane = iota((16, LANES), 1)
    at_first, at_last = lane == 0, lane == LANES - 1

    def gather_end(side, z, k, value, total_so_far):
        j = z * len(pairs) + k
        shift = j if side == 0 else lax.rem(j + 1, LANES)
        return jnp.where(lane == j, pltpu.roll(value, shift, 1), total_so_far)

    zero = jnp.zeros((16, LANES), BF16)

    def settle(n, ends):
        ends = list(ends)
        placing = one_hot(iota((cells, total), 0) + n * cells == slots_row)
        for c in range(3):
            push = jnp.dot(placing, force_ref[c], preferred_element_type=F32)
            for k in range(chunk):
                z = n * chunk + k
                for t in range(tiles):
                    value = fluid_ref[t, c, z] + push[
                        k * rows:(k + 1) * rows, t * LANES:(t + 1) * LANES]
                    first_ref[c, t, z, PAD:PAD + rows, :] = value
                    for n_pair, pair in enumerate(pairs):
                        packed = jnp.concatenate(
                            [value[8 * g:8 * g + 8] for g in pair], axis=0).astype(BF16)
                        first_half[c, t, z, 16 * n_pair:16 * n_pair + 16, :] = packed
                        for side in range(2):
                            if t == side * (tiles - 1):
                                n_end = side * 3 + c
                                ends[n_end] = gather_end(
                                    side, z, n_pair, packed, ends[n_end])
        return tuple(ends)

    has = [gx > 0, gx < rows_grid - 1, gy > 0, gy < columns_grid - 1]

    def copies_of(step, wanted=range(4)):
        plan = [
            (sides_send.at[step, 0], sides_recv.at[step, 1], (-1, 0), has[0], has[1]),
            (sides_send.at[step, 1], sides_recv.at[step, 0], (1, 0), has[1], has[0]),
            (ends_send.at[step, 0], ends_recv.at[step, 1], (0, -1), has[2], has[3]),
            (ends_send.at[step, 1], ends_recv.at[step, 0], (0, 1), has[3], has[2]),
        ]
        out = []
        for n, (source, target, (dx, dy), sends, receives) in enumerate(plan):
            if n not in wanted:
                continue
            to = (lax.rem(gx + dx + rows_grid, rows_grid),
                  lax.rem(gy + dy + columns_grid, columns_grid))
            out.append((pltpu.make_async_remote_copy(
                src_ref=source, dst_ref=target, send_sem=hsend_sem.at[step, n],
                recv_sem=hrecv_sem.at[step, n], device_id=to, device_id_type=MESH),
                sends, receives))
        return out

    def send_halo(step, ref, ends):
        flat = ref.reshape(flat_shape)
        for side in range(2):
            row = PAD + side * (rows - 1)
            for c in range(3):
                for t in range(tiles):
                    sides_send[step, side, c, t] = jnp.concatenate(
                        [flat[c, t, pl.ds(g * stride + row, 8, stride=stride), :]
                         for g in range(0, layers, 8)], axis=0).astype(BF16)
        for side in range(2):
            for c in range(3):
                ends_send[step, side, c] = ends[side * 3 + c]
        for copy, sends, _ in copies_of(step):
            @pl.when(sends)
            def _():
                copy.start()

    def wait_ends(step):
        for copy, _, receives in copies_of(step, (2, 3)):
            @pl.when(receives)
            def _():
                copy.wait_recv()
        for side in range(2):
            for c in range(3):
                halo_ref[side, c] = jnp.where(
                    has[2 + side], ends_recv[step, side, c].astype(F32), 0.0).astype(BF16)

    def wait_sides(step, ref):
        flat = ref.reshape(flat_shape)
        for copy, _, receives in copies_of(step, (0, 1)):
            @pl.when(receives)
            def _():
                copy.wait_recv()
        for side in range(2):
            row = PAD - 1 if side == 0 else PAD + rows
            for c in range(3):
                for t in range(tiles):
                    value = jnp.where(has[side], sides_recv[step, side, c, t].astype(F32), 0.0)
                    for g in range(0, layers, 8):
                        flat[c, t, pl.ds(g * stride + row, 8, stride=stride), :] = value[g:g + 8]

    def sweep_tiles(ref, half, z, k):
        up, down = lax.rem(z + 1, layers), lax.rem(z + layers - 1, layers)
        j = z * len(pairs) + k
        at = slice(16 * k, 16 * k + 16)

        def beside(c, t, offset):
            return jnp.concatenate(
                [ref[c, t, z, PAD + 8 * g + offset:PAD + 8 * g + offset + 8, :]
                 for g in pairs[k]], axis=0)

        whole = [[beside(c, t, 0) for t in range(tiles)] for c in range(3)]
        mids = [[v.astype(BF16) for v in row] for row in whole]
        right, left = [], []
        for c in range(3):
            right.append([pltpu.roll(halo_ref[0, c], lax.rem(LANES - j, LANES), 1)]
                         + [pltpu.roll(v, 1, 1) for v in mids[c]])
            left.append([pltpu.roll(v, LANES - 1, 1) for v in mids[c]]
                        + [pltpu.roll(halo_ref[1, c], LANES - 1 - j, 1)])
        for t in range(tiles):
            parts = []
            for c in range(3):
                parts.append((
                    mids[c][t], beside(c, t, 1).astype(BF16), beside(c, t, -1).astype(BF16),
                    jnp.where(at_last, left[c][t + 1], left[c][t]),
                    jnp.where(at_first, right[c][t], right[c][t + 1]),
                    half[c, t, up, at, :], half[c, t, down, at, :]))
            change = sweep(*[list(v) for v in zip(*parts)])
            yield t, [keep * whole[c][t] + transport_rate * change[c].astype(F32)
                      for c in range(3)]

    def run(step, ref, half, store, ends):
        def body(wanted, i, ends):
            ends = list(ends)
            for m in range(unroll):
                z = i * unroll + m
                for k in wanted:
                    for t, new in sweep_tiles(ref, half, z, k):
                        for c in range(3):
                            packed = store(c, t, z, k, new[c])
                            if step == 0 and t in (0, tiles - 1):
                                n_end = (0 if t == 0 else 3) + c
                                ends[n_end] = gather_end(t > 0, z, k, packed, ends[n_end])
            return tuple(ends)

        count = layers // unroll
        wait_ends(step)
        ends = lax.fori_loop(
            0, count, functools.partial(body, range(len(pairs) - 1)), ends)
        wait_sides(step, ref)
        return lax.fori_loop(0, count, functools.partial(body, (len(pairs) - 1,)), ends)

    ends = lax.fori_loop(0, layers // chunk, settle, (zero,) * 6)
    send_halo(0, first_ref, ends)
    slots = table_column(table_ref, per_owner)
    taking_ref[...] = one_hot(iota((total, layers * rows), 1) == slots)

    def store_first(c, t, z, k, value):
        for m, g in enumerate(pairs[k]):
            second_ref[c, t, z, PAD + 8 * g:PAD + 8 * g + 8, :] = value[8 * m:8 * m + 8]
        packed = value.astype(BF16)
        second_half[c, t, z, 16 * k:16 * k + 16, :] = packed
        return packed

    ends = run(0, first_ref, first_half, store_first, (zero,) * 6)
    send_halo(1, second_ref, ends)

    def store_second(c, t, z, k, value):
        for m, g in enumerate(pairs[k]):
            fluid_ref[t, c, z, 8 * g:8 * g + 8, :] = value[8 * m:8 * m + 8]

    run(1, second_ref, second_half, store_second, (zero,) * 6)

    width = 3 * tiles * per_owner
    for c in range(3):
        for h in range(0, tiles, 2):
            flat = jnp.concatenate(
                [fluid_ref[h + s, c].reshape(layers * rows, LANES).astype(BF16)
                 for s in range(2)], axis=1)
            part = jnp.dot(taking_ref[...], flat, preferred_element_type=F32)
            for p in range(per_owner):
                for s in range(2):
                    stage_ref[pl.ds(p * 3 * tiles + c * tiles + h + s, devices, stride=width), :] = (
                        part[p * devices:(p + 1) * devices, s * LANES:(s + 1) * LANES])
    replies_ref[...] = stage_ref[...].reshape(replies_ref.shape).astype(BF16)
    wait = start_swap(
        columns_grid, devices, [replies_ref], [returned_ref], rsend_sem, rrecv_sem, rown_sem)
    for step in range(STEPS):
        for copy, sends, _ in copies_of(step):
            @pl.when(sends)
            def _():
                copy.wait_send()
    owner_row = to_row(owners_ref[:, 0, :])
    places = slot_column(owner_row, to_column(owner_row), devices)
    selector = one_hot(iota((places.shape[0], total), 1) == places)
    wait()
    interpolate(
        devices, per_owner, returned_ref, loaded_ref, selector, stage_ref, picked_ref, interp_ref)


def interpolate(
    devices, per_owner, returned_ref, loaded_ref, selector, stage_ref, picked_ref, interp_ref,
):
    blocks, k, points, patch = loaded_ref.shape
    tiles = patch // LANES
    stage_ref[...] = returned_ref[...].astype(F32).reshape(stage_ref.shape)
    for c in range(3):
        replies = unpack(stage_ref, devices, per_owner, tiles, c).astype(BF16)
        picked_ref[c] = jnp.dot(selector, replies, preferred_element_type=F32)
    diagonal = iota((k, k * points), 0) == iota((k, k * points), 1) // points
    for b in range(blocks):
        rows = [picked_ref[c, b * k:(b + 1) * k, :] for c in range(3)]
        rows.append(jnp.zeros_like(rows[0]))
        left = jnp.concatenate(rows, axis=0).astype(BF16)
        right = loaded_ref[b].reshape(k * points, patch)
        result = lax.dot_general(
            left, right, (((1,), (1,)), ((), ())), preferred_element_type=F32)
        for c in range(3):
            own = jnp.where(diagonal, result[c * k:(c + 1) * k], 0.0)
            fold = own[:, 0:points]
            for n in range(1, k):
                fold = fold + own[:, n * points:(n + 1) * points]
            interp_ref[c, b:b + 1, :] = jnp.sum(fold, axis=0, keepdims=True)


def finish_kernel(fluid_ref, interp_ref, points_ref, out_ref, moved_ref, store_sem):
    def store(t):
        return pltpu.make_async_copy(
            fluid_ref.at[t], out_ref.at[:, :, :, pl.ds(t * LANES, LANES)], store_sem.at[t])

    for t in range(fluid_ref.shape[0]):
        store(t).start()
    moved_ref[...] = points_ref[...] + fiber_step * interp_ref[...]
    for t in range(fluid_ref.shape[0]):
        store(t).wait()


def shards(rows_grid, columns_grid, velocity, fiber_points, stiffness, links, delta_weights,
           owners, patch_slots):
    blocks, intersection, points, patch = delta_weights.shape
    _, layers, rows, columns = velocity.shape
    devices = rows_grid * columns_grid
    entries = blocks * intersection
    per_owner = max(2, (2 * entries + devices - 1) // devices)
    total = devices * per_owner
    tiles = patch // LANES
    width = 3 * tiles * per_owner
    owners = jnp.transpose(owners, (0, 2, 1))
    points_first = jnp.transpose(fiber_points, (1, 0, 2))
    message = jax.ShapeDtypeStruct((devices, width, LANES), BF16)
    table_shape = jax.ShapeDtypeStruct((devices, 1, LANES), I32)
    stage = pltpu.VMEM((devices * width, LANES), F32)
    limit = 46 << 20
    field = pltpu.VMEM((3, tiles, layers, rows + 2 * PAD, LANES), F32)
    half = pltpu.VMEM((3, tiles, layers, rows, LANES), BF16)
    sides = pltpu.VMEM((STEPS, 2, 3, tiles, layers, LANES), BF16)
    ends = pltpu.VMEM((STEPS, 2, 3, 16, LANES), BF16)
    fluid_tiles, interp = pl.pallas_call(
        functools.partial(step_kernel, rows_grid, columns_grid, per_owner, UNROLL),
        out_shape=[
            jax.ShapeDtypeStruct((tiles, 3, layers, rows, LANES), F32),
            jax.ShapeDtypeStruct(points_first.shape, F32),
        ],
        in_specs=[HBM] * 7,
        out_specs=[VMEM] * 2,
        scratch_shapes=[
            pltpu.VMEM(delta_weights.shape, BF16),
            pltpu.VMEM(message.shape, BF16),
            pltpu.VMEM((3, entries, patch), F32),
            pltpu.VMEM(points_first.shape, F32),
            pltpu.SMEM(stiffness.shape, F32),
            pltpu.VMEM(links.shape, I32),
            pltpu.VMEM(owners.shape, I32),
            pltpu.VMEM(patch_slots.shape, I32),
            pltpu.SemaphoreType.DMA((5,)),
            pltpu.VMEM(message.shape, BF16),
            pltpu.VMEM(table_shape.shape, I32),
            pltpu.VMEM(message.shape, BF16),
            pltpu.VMEM(table_shape.shape, I32),
            pltpu.VMEM(message.shape, BF16),
            pltpu.VMEM((3, entries, patch), F32),
            stage,
            pltpu.VMEM((3, total, patch), BF16),
            field, field, half, half,
            pltpu.VMEM((total, layers * rows), BF16),
            sides, sides, ends, ends,
            pltpu.VMEM((2, 3, 16, LANES), BF16),
            *swap_sems(2, devices),
            *swap_sems(1, devices),
            pltpu.SemaphoreType.DMA((tiles,)),
            pltpu.SemaphoreType.DMA((blocks,)),
            pltpu.SemaphoreType.DMA((STEPS, 4)),
            pltpu.SemaphoreType.DMA((STEPS, 4)),
        ],
        compiler_params=pltpu.CompilerParams(
            collective_id=0, has_side_effects=True, vmem_limit_bytes=limit),
    )(*[pltpu.with_memory_space_constraint(v, pltpu.HBM) for v in (
        points_first, stiffness, links, owners, patch_slots, delta_weights, velocity)])

    fluid, moved = pl.pallas_call(
        finish_kernel,
        out_shape=[
            jax.ShapeDtypeStruct(velocity.shape, F32),
            jax.ShapeDtypeStruct(points_first.shape, F32),
        ],
        in_specs=[VMEM] * 3,
        out_specs=[HBM, VMEM],
        scratch_shapes=[pltpu.SemaphoreType.DMA((tiles,))],
        compiler_params=pltpu.CompilerParams(vmem_limit_bytes=limit),
    )(fluid_tiles, interp, points_first)
    return fluid, jnp.transpose(moved, (1, 0, 2))


def solution(mesh):
    placed = (
        P(None, None, "gx", "gy"),
        P(("gx", "gy"), None, None),
        P(("gx", "gy")),
        P(("gx", "gy"), None),
        P(("gx", "gy"), None, None, None),
        P(("gx", "gy"), None, None),
        P(("gx", "gy"), None),
    )
    return jax.shard_map(
        functools.partial(shards, mesh.shape["gx"], mesh.shape["gy"]),
        mesh=mesh,
        in_specs=placed,
        out_specs=(placed[0], placed[1]),
        check_vma=False,
    )
```

profile of v0, /device:TPU:0, one launch (start us, length us, event | category | flops | bytes accessed | tf_op | source)
XLA Modules:
  0.0 58.9 jit_solution(7658276844328325460)
XLA Ops:
  0.6 0.0 copy-start
  0.6 54.9 %shard_map.86 = (f32[4,3,32,32,128]{4,3,2,1,0:T(8,128)S(1)}, f32[3,8,128]{2,1,0:T(8,128)S(1)}) custom-call(f32[3,8,128]{2,1,0:T(8,128)} %bitcast.5, f32[8]{0:T(128)} %stiffness_in.1, s32[8,128]{1,0:T(8,128)} %links_in.1, s32[8,1,8]{2,1,0:T(1,128)} %bitcast.7, s32[8,8]{1,0:T(8,128)} %slots_in.1, bf16[8,8,128,512]{3,2,1,0:T(8,128)(2,1)} %weights_ref.1, ...), custom_call_target="tpu_custom_call" | custom-call | tf_op jit(solution)/shard_map/pallas_call | solution.py:536
  55.5 0.0 copy-done
  55.5 3.3 %shard_map.87 = (f32[3,32,32,512]{3,2,1,0:T(8,128)}, f32[3,8,128]{2,1,0:T(8,128)}) custom-call(f32[4,3,32,32,128]{4,3,2,1,0:T(8,128)S(1)} %get-tuple-element.6.fluid_ref, f32[3,8,128]{2,1,0:T(8,128)S(1)} %get-tuple-element.7.interp_ref, f32[3,8,128]{2,1,0:T(8,128)S(1)} %bitcast.6), custom_call_target="tpu_custom_call" | custom-call | tf_op jit(solution)/shard_map/pallas_call | solution.py:578
Async XLA Ops:
  0.6 54.9 %copy-start = (f32[8,3,128]{2,0,1:T(8,128)S(1)}, f32[8,3,128]{2,0,1:T(8,128)}, u32[]{:S(2)}) copy-start(f32[8,3,128]{2,0,1:T(8,128)} %param.8) | copy-start | bytes 36868
where the time goes:
time: 59 us; the launch traced here: 58.9 us
  Pallas kernels  58.2 us (99%)
  between operations  0.66 us (1%)
    pallas_call x1, Pallas kernels, shards(): pl.pallas_call(functools.partial(step_kernel, rows_grid, columns_grid, pe...  54.9 us
    pallas_call x1, Pallas kernels, shards(): pl.pallas_call(finish_kernel, out_shape=[jax.ShapeDtypeStruct(velocity.sh...  3.33 us

commit v1 on v0

--- a/solution.py
+++ b/solution.py
@@ -118,53 +118,40 @@
 HBM = pl.BlockSpec(memory_space=pltpu.HBM)
 
 
-def place(d, columns):
-    return (d // columns, lax.rem(d, columns))
-
-
-def start_swap(columns, devices, ins, outs, send_sem, recv_sem, own_sem):
-    count = len(ins)
-    me = lax.axis_index("gx") * columns + lax.axis_index("gy")
-
-    def copy(n, off):
-        other = lax.rem(me + off, devices)
-        return pltpu.make_async_remote_copy(
-            src_ref=ins[n].at[other], dst_ref=outs[n].at[me],
-            send_sem=send_sem.at[n, off], recv_sem=recv_sem.at[n, off],
-            device_id=place(other, columns), device_id_type=MESH,
-        )
-
-    def start(off, carry):
-        for n in range(count):
-            copy(n, off).start()
+def each_peer(rows_grid, columns_grid, visit, carry=0):
+    gx, gy = lax.axis_index("gx"), lax.axis_index("gy")
+    ys = [lax.rem(gy + dy, columns_grid) for dy in range(columns_grid)]
+    for dy in range(1, columns_grid):
+        visit(dy, (gx, ys[dy]))
+
+    def row(dx, carry):
+        x = lax.rem(gx + dx, rows_grid)
+        for dy in range(columns_grid):
+            visit(dx * columns_grid + dy, (x, ys[dy]))
         return carry
 
-    def finish(off, carry):
-        for n in range(count):
-            copy(n, off).wait()
-        return carry
-
-    def own(n):
-        return pltpu.make_async_copy(ins[n].at[me], outs[n].at[me], own_sem.at[n])
-
-    lax.fori_loop(1, devices, start, 0)
-    for n in range(count):
-        own(n).start()
+    lax.fori_loop(1, rows_grid, row, 0)
+
+
+def start_swap(rows_grid, columns_grid, source, target, send_sem, recv_sem):
+    devices = rows_grid * columns_grid
+    me = lax.axis_index("gx") * columns_grid + lax.axis_index("gy")
+
+    def start(off, to):
+        pltpu.make_async_remote_copy(
+            src_ref=source.at[to[0] * columns_grid + to[1]], dst_ref=target.at[me],
+            send_sem=send_sem, recv_sem=recv_sem, device_id=to, device_id_type=MESH,
+        ).start()
+
+    each_peer(rows_grid, columns_grid, start)
+    pltpu.make_async_copy(source.at[me], target.at[me], recv_sem).start()
 
     def wait():
-        for n in range(count):
-            own(n).wait()
-        lax.fori_loop(1, devices, finish, 0)
+        sent = pl.ds(0, devices - 1)
+        pltpu.make_async_copy(source, target, recv_sem).wait()
+        pltpu.make_async_copy(source.at[sent], target.at[sent], send_sem).wait()
 
     return wait
-
-
-def swap_sems(count, devices):
-    return [
-        pltpu.SemaphoreType.DMA((count, devices)),
-        pltpu.SemaphoreType.DMA((count, devices)),
-        pltpu.SemaphoreType.DMA((count,)),
-    ]
 
 
 def unpack(stage_ref, devices, per_owner, tiles, c):
@@ -215,12 +202,12 @@
 
 
 def step_kernel(
-    rows_grid, columns_grid, per_owner, unroll, points_in, stiffness_in, links_in, owners_in,
+    rows_grid, columns_grid, per_owner, points_in, stiffness_in, links_in, owners_in,
     slots_in, weights_ref, velocity_ref,
-    fluid_ref, interp_ref, loaded_ref, returned_ref, picked_ref,
+    fluid_ref, loaded_ref, returned_ref,
     points_ref, stiffness_ref, links_ref, owners_ref, slots_ref, small_sem, received_ref, table_ref, out_ref, outtable_ref, replies_ref, contrib_ref, stage_ref,
     force_ref, first_ref, second_ref, first_half, second_half, taking_ref, sides_send, sides_recv, ends_send, ends_recv,
-    halo_ref, send_sem, recv_sem, own_sem, rsend_sem, rrecv_sem, rown_sem, load_sem, block_sem,
+    halo_ref, send_sem, recv_sem, load_sem, block_sem,
     hsend_sem, hrecv_sem,
 ):
     devices = rows_grid * columns_grid
@@ -249,32 +236,34 @@
     for copy in small:
         copy.start()
     for b in range(blocks):
-        block(b).start()
-    for t in range(tiles):
-        load(t).start()
+        block(b).start(priority=1)
+
+    def wait_block(b):
+        block(b).wait()
+        if b == blocks - 1:
+            for t in range(tiles):
+                load(t).start()
 
     gx, gy = lax.axis_index("gx"), lax.axis_index("gy")
-    me = gx * columns_grid + gy
     barrier = pltpu.get_barrier_semaphore()
 
-    def hello(off, carry):
-        other = lax.rem(me + off, devices)
-        pl.semaphore_signal(
-            barrier, inc=1, device_id=place(other, columns_grid), device_id_type=MESH)
-        return carry
-
-    lax.fori_loop(1, devices, hello, 0)
+    def hello(off, to):
+        pl.semaphore_signal(barrier, inc=1, device_id=to, device_id_type=MESH)
+
+    each_peer(rows_grid, columns_grid, hello)
     for copy in small:
         copy.wait()
     spread(
         devices, per_owner, points_ref, stiffness_ref, links_ref, owners_ref, slots_ref,
-        loaded_ref, out_ref, outtable_ref, contrib_ref, stage_ref, lambda b: block(b).wait())
+        loaded_ref, out_ref, outtable_ref, contrib_ref, stage_ref, wait_block)
     pl.semaphore_wait(barrier, devices - 1)
+    wait_table = start_swap(
+        rows_grid, columns_grid, outtable_ref, table_ref, send_sem.at[0], recv_sem.at[0])
     wait = start_swap(
-        columns_grid, devices, [out_ref, outtable_ref], [received_ref, table_ref],
-        send_sem, recv_sem, own_sem)
+        rows_grid, columns_grid, out_ref, received_ref, send_sem.at[1], recv_sem.at[1])
     for t in range(tiles):
         load(t).wait()
+    wait_table()
     wait()
 
     stage_ref[...] = received_ref[...].astype(F32).reshape(stage_ref.shape)
@@ -286,10 +275,11 @@
     lane = iota((16, LANES), 1)
     at_first, at_last = lane == 0, lane == LANES - 1
 
-    def gather_end(side, z, k, value, total_so_far):
-        j = z * len(pairs) + k
+    unit = one_hot(at_first)
+
+    def gather_end(side, mark, j, value, total_so_far):
         shift = j if side == 0 else lax.rem(j + 1, LANES)
-        return jnp.where(lane == j, pltpu.roll(value, shift, 1), total_so_far)
+        return total_so_far + mark * pltpu.roll(value, shift, 1)
 
     zero = jnp.zeros((16, LANES), BF16)
 
@@ -311,8 +301,9 @@
                         for side in range(2):
                             if t == side * (tiles - 1):
                                 n_end = side * 3 + c
+                                j = z * len(pairs) + n_pair
                                 ends[n_end] = gather_end(
-                                    side, z, n_pair, packed, ends[n_end])
+                                    side, pltpu.roll(unit, j, 1), j, packed, ends[n_end])
         return tuple(ends)
 
     has = [gx > 0, gx < rows_grid - 1, gy > 0, gy < columns_grid - 1]
@@ -377,7 +368,7 @@
                     for g in range(0, layers, 8):
                         flat[c, t, pl.ds(g * stride + row, 8, stride=stride), :] = value[g:g + 8]
 
-    def sweep_tiles(ref, half, z, k):
+    def sweep_tiles(ref, half, z, k, wanted):
         up, down = lax.rem(z + 1, layers), lax.rem(z + layers - 1, layers)
         j = z * len(pairs) + k
         at = slice(16 * k, 16 * k + 16)
@@ -389,45 +380,52 @@
 
         whole = [[beside(c, t, 0) for t in range(tiles)] for c in range(3)]
         mids = [[v.astype(BF16) for v in row] for row in whole]
-        right, left = [], []
-        for c in range(3):
-            right.append([pltpu.roll(halo_ref[0, c], lax.rem(LANES - j, LANES), 1)]
-                         + [pltpu.roll(v, 1, 1) for v in mids[c]])
-            left.append([pltpu.roll(v, LANES - 1, 1) for v in mids[c]]
-                        + [pltpu.roll(halo_ref[1, c], LANES - 1 - j, 1)])
-        for t in range(tiles):
+        turned = {}
+
+        def turn(c, t, shift):
+            if (c, t, shift) not in turned:
+                if t < 0:
+                    v = pltpu.roll(halo_ref[0, c], lax.rem(LANES - j, LANES), 1)
+                elif t == tiles:
+                    v = pltpu.roll(halo_ref[1, c], LANES - 1 - j, 1)
+                else:
+                    v = pltpu.roll(mids[c][t], shift, 1)
+                turned[c, t, shift] = v
+            return turned[c, t, shift]
+
+        for t in wanted:
             parts = []
             for c in range(3):
                 parts.append((
                     mids[c][t], beside(c, t, 1).astype(BF16), beside(c, t, -1).astype(BF16),
-                    jnp.where(at_last, left[c][t + 1], left[c][t]),
-                    jnp.where(at_first, right[c][t], right[c][t + 1]),
+                    jnp.where(at_last, turn(c, t + 1, LANES - 1), turn(c, t, LANES - 1)),
+                    jnp.where(at_first, turn(c, t - 1, 1), turn(c, t, 1)),
                     half[c, t, up, at, :], half[c, t, down, at, :]))
             change = sweep(*[list(v) for v in zip(*parts)])
             yield t, [keep * whole[c][t] + transport_rate * change[c].astype(F32)
                       for c in range(3)]
 
-    def run(step, ref, half, store, ends):
-        def body(wanted, i, ends):
+    def run(ref, half, store, edge, groups_wanted, tiles_wanted, unroll, ends):
+        def body(i, ends):
             ends = list(ends)
             for m in range(unroll):
                 z = i * unroll + m
-                for k in wanted:
-                    for t, new in sweep_tiles(ref, half, z, k):
+                for k in groups_wanted:
+                    j = z * len(pairs) + k
+                    mark = pltpu.roll(unit, j, 1)
+                    for t, new in sweep_tiles(ref, half, z, k, tiles_wanted):
                         for c in range(3):
                             packed = store(c, t, z, k, new[c])
-                            if step == 0 and t in (0, tiles - 1):
+                            if edge and t in (0, tiles - 1):
                                 n_end = (0 if t == 0 else 3) + c
-                                ends[n_end] = gather_end(t > 0, z, k, packed, ends[n_end])
+                                ends[n_end] = gather_end(t > 0, mark, j, packed, ends[n_end])
             return tuple(ends)
 
-        count = layers // unroll
-        wait_ends(step)
-        ends = lax.fori_loop(
-            0, count, functools.partial(body, range(len(pairs) - 1)), ends)
-        wait_sides(step, ref)
-        return lax.fori_loop(0, count, functools.partial(body, (len(pairs) - 1,)), ends)
-
+        return lax.fori_loop(0, layers // unroll, body, ends)
+
+    inner, outer = range(len(pairs) - 1), (len(pairs) - 1,)
+    every = range(tiles)
+    ends_zero = (zero,) * 6
     ends = lax.fori_loop(0, layers // chunk, settle, (zero,) * 6)
     send_halo(0, first_ref, ends)
     slots = table_column(table_ref, per_owner)
@@ -440,51 +438,66 @@
         second_half[c, t, z, 16 * k:16 * k + 16, :] = packed
         return packed
 
-    ends = run(0, first_ref, first_half, store_first, (zero,) * 6)
+    wait_ends(0)
+    ends = run(first_ref, first_half, store_first, True, inner, every, UNROLL, ends_zero)
+    wait_sides(0, first_ref)
+    ends = run(first_ref, first_half, store_first, True, outer, every, UNROLL, ends)
     send_halo(1, second_ref, ends)
 
     def store_second(c, t, z, k, value):
         for m, g in enumerate(pairs[k]):
             fluid_ref[t, c, z, 8 * g:8 * g + 8, :] = value[8 * m:8 * m + 8]
 
-    run(1, second_ref, second_half, store_second, (zero,) * 6)
-
-    width = 3 * tiles * per_owner
-    for c in range(3):
-        for h in range(0, tiles, 2):
+    half_tiles = tiles // 2
+    wide = replies_ref.shape[2]
+    wait_ends(1)
+    waits = []
+    for h in range(2):
+        mine = range(h * half_tiles, (h + 1) * half_tiles)
+        run(second_ref, second_half, store_second, False, inner, mine, 2 * UNROLL, ())
+        if h == 0:
+            wait_sides(1, second_ref)
+        run(second_ref, second_half, store_second, False, outer, mine, 2 * UNROLL, ())
+        for c in range(3):
             flat = jnp.concatenate(
-                [fluid_ref[h + s, c].reshape(layers * rows, LANES).astype(BF16)
-                 for s in range(2)], axis=1)
+                [fluid_ref[t, c].reshape(layers * rows, LANES).astype(BF16) for t in mine], axis=1)
             part = jnp.dot(taking_ref[...], flat, preferred_element_type=F32)
             for p in range(per_owner):
-                for s in range(2):
-                    stage_ref[pl.ds(p * 3 * tiles + c * tiles + h + s, devices, stride=width), :] = (
-                        part[p * devices:(p + 1) * devices, s * LANES:(s + 1) * LANES])
-    replies_ref[...] = stage_ref[...].reshape(replies_ref.shape).astype(BF16)
-    wait = start_swap(
-        columns_grid, devices, [replies_ref], [returned_ref], rsend_sem, rrecv_sem, rown_sem)
+                for n in range(half_tiles):
+                    row = (p * 3 + c) * half_tiles + n
+                    stage_ref[pl.ds(row, devices, stride=wide), :] = (
+                        part[p * devices:(p + 1) * devices, n * LANES:(n + 1) * LANES])
+        replies_ref[h] = stage_ref[0:devices * wide, :].reshape(replies_ref.shape[1:]).astype(BF16)
+        waits.append(start_swap(
+            rows_grid, columns_grid, replies_ref.at[h], returned_ref.at[h],
+            send_sem.at[2 + h], recv_sem.at[2 + h]))
     for step in range(STEPS):
         for copy, sends, _ in copies_of(step):
             @pl.when(sends)
             def _():
                 copy.wait_send()
-    owner_row = to_row(owners_ref[:, 0, :])
-    places = slot_column(owner_row, to_column(owner_row), devices)
-    selector = one_hot(iota((places.shape[0], total), 1) == places)
-    wait()
-    interpolate(
-        devices, per_owner, returned_ref, loaded_ref, selector, stage_ref, picked_ref, interp_ref)
+    for wait in waits:
+        wait()
 
 
 def interpolate(
-    devices, per_owner, returned_ref, loaded_ref, selector, stage_ref, picked_ref, interp_ref,
+    devices, per_owner, returned_ref, loaded_ref, selector, stage_ref, picked_ref, points_ref, moved_ref,
 ):
     blocks, k, points, patch = loaded_ref.shape
     tiles = patch // LANES
-    stage_ref[...] = returned_ref[...].astype(F32).reshape(stage_ref.shape)
-    for c in range(3):
-        replies = unpack(stage_ref, devices, per_owner, tiles, c).astype(BF16)
-        picked_ref[c] = jnp.dot(selector, replies, preferred_element_type=F32)
+    half_tiles = tiles // 2
+    wide = returned_ref.shape[2]
+    for h in range(2):
+        stage_ref[0:devices * wide, :] = returned_ref[h].astype(F32).reshape(
+            devices * wide, LANES)
+        for c in range(3):
+            replies = jnp.concatenate(
+                [jnp.concatenate(
+                    [stage_ref[pl.ds((p * 3 + c) * half_tiles + n, devices, stride=wide), :]
+                     for n in range(half_tiles)], axis=1)
+                 for p in range(per_owner)], axis=0).astype(BF16)
+            picked_ref[c, :, h * half_tiles * LANES:(h + 1) * half_tiles * LANES] = jnp.dot(
+                selector, replies, preferred_element_type=F32)
     diagonal = iota((k, k * points), 0) == iota((k, k * points), 1) // points
     for b in range(blocks):
         rows = [picked_ref[c, b * k:(b + 1) * k, :] for c in range(3)]
@@ -498,17 +511,34 @@
             fold = own[:, 0:points]
             for n in range(1, k):
                 fold = fold + own[:, n * points:(n + 1) * points]
-            interp_ref[c, b:b + 1, :] = jnp.sum(fold, axis=0, keepdims=True)
-
-
-def finish_kernel(fluid_ref, interp_ref, points_ref, out_ref, moved_ref, store_sem):
+            interp = jnp.sum(fold, axis=0, keepdims=True)
+            moved_ref[c, b:b + 1, :] = points_ref[c, b:b + 1, :] + fiber_step * interp
+
+
+def finish_kernel(
+    devices, per_owner, fluid_ref, loaded_ref, returned_ref, owners_in, points_in,
+    out_ref, moved_ref, owners_ref, points_ref, stage_ref, picked_ref, small_sem, store_sem,
+):
     def store(t):
         return pltpu.make_async_copy(
             fluid_ref.at[t], out_ref.at[:, :, :, pl.ds(t * LANES, LANES)], store_sem.at[t])
 
+    small = [
+        pltpu.make_async_copy(owners_in, owners_ref, small_sem.at[0]),
+        pltpu.make_async_copy(points_in, points_ref, small_sem.at[1]),
+    ]
+    for copy in small:
+        copy.start()
     for t in range(fluid_ref.shape[0]):
         store(t).start()
-    moved_ref[...] = points_ref[...] + fiber_step * interp_ref[...]
+    for copy in small:
+        copy.wait()
+    owner_row = to_row(owners_ref[:, 0, :])
+    places = slot_column(owner_row, to_column(owner_row), devices)
+    selector = one_hot(iota((places.shape[0], devices * per_owner), 1) == places)
+    interpolate(
+        devices, per_owner, returned_ref, loaded_ref, selector, stage_ref, picked_ref, points_ref,
+        moved_ref)
     for t in range(fluid_ref.shape[0]):
         store(t).wait()
 
@@ -526,25 +556,25 @@
     owners = jnp.transpose(owners, (0, 2, 1))
     points_first = jnp.transpose(fiber_points, (1, 0, 2))
     message = jax.ShapeDtypeStruct((devices, width, LANES), BF16)
+    wide = -(-3 * (tiles // 2) * per_owner // 8) * 8
+    reply = jax.ShapeDtypeStruct((2, devices, wide, LANES), BF16)
     table_shape = jax.ShapeDtypeStruct((devices, 1, LANES), I32)
-    stage = pltpu.VMEM((devices * width, LANES), F32)
-    limit = 46 << 20
+    stage = pltpu.VMEM((devices * max(width, wide), LANES), F32)
+    limit = 32 << 20
     field = pltpu.VMEM((3, tiles, layers, rows + 2 * PAD, LANES), F32)
     half = pltpu.VMEM((3, tiles, layers, rows, LANES), BF16)
     sides = pltpu.VMEM((STEPS, 2, 3, tiles, layers, LANES), BF16)
     ends = pltpu.VMEM((STEPS, 2, 3, 16, LANES), BF16)
-    fluid_tiles, interp = pl.pallas_call(
-        functools.partial(step_kernel, rows_grid, columns_grid, per_owner, UNROLL),
+    fluid_tiles, weights, returned = pl.pallas_call(
+        functools.partial(step_kernel, rows_grid, columns_grid, per_owner),
         out_shape=[
             jax.ShapeDtypeStruct((tiles, 3, layers, rows, LANES), F32),
-            jax.ShapeDtypeStruct(points_first.shape, F32),
+            jax.ShapeDtypeStruct(delta_weights.shape, BF16),
+            reply,
         ],
         in_specs=[HBM] * 7,
-        out_specs=[VMEM] * 2,
+        out_specs=[VMEM] * 3,
         scratch_shapes=[
-            pltpu.VMEM(delta_weights.shape, BF16),
-            pltpu.VMEM(message.shape, BF16),
-            pltpu.VMEM((3, entries, patch), F32),
             pltpu.VMEM(points_first.shape, F32),
             pltpu.SMEM(stiffness.shape, F32),
             pltpu.VMEM(links.shape, I32),
@@ -555,7 +585,7 @@
             pltpu.VMEM(table_shape.shape, I32),
             pltpu.VMEM(message.shape, BF16),
             pltpu.VMEM(table_shape.shape, I32),
-            pltpu.VMEM(message.shape, BF16),
+            pltpu.VMEM(reply.shape, BF16),
             pltpu.VMEM((3, entries, patch), F32),
             stage,
             pltpu.VMEM((3, total, patch), BF16),
@@ -563,8 +593,8 @@
             pltpu.VMEM((total, layers * rows), BF16),
             sides, sides, ends, ends,
             pltpu.VMEM((2, 3, 16, LANES), BF16),
-            *swap_sems(2, devices),
-            *swap_sems(1, devices),
+            pltpu.SemaphoreType.DMA((4,)),
+            pltpu.SemaphoreType.DMA((4,)),
             pltpu.SemaphoreType.DMA((tiles,)),
             pltpu.SemaphoreType.DMA((blocks,)),
             pltpu.SemaphoreType.DMA((STEPS, 4)),
@@ -576,16 +606,24 @@
         points_first, stiffness, links, owners, patch_slots, delta_weights, velocity)])
 
     fluid, moved = pl.pallas_call(
-        finish_kernel,
+        functools.partial(finish_kernel, devices, per_owner),
         out_shape=[
             jax.ShapeDtypeStruct(velocity.shape, F32),
             jax.ShapeDtypeStruct(points_first.shape, F32),
         ],
-        in_specs=[VMEM] * 3,
+        in_specs=[VMEM, VMEM, VMEM, HBM, HBM],
         out_specs=[HBM, VMEM],
-        scratch_shapes=[pltpu.SemaphoreType.DMA((tiles,))],
-        compiler_params=pltpu.CompilerParams(vmem_limit_bytes=limit),
-    )(fluid_tiles, interp, points_first)
+        scratch_shapes=[
+            pltpu.VMEM(owners.shape, I32),
+            pltpu.VMEM(points_first.shape, F32),
+            stage,
+            pltpu.VMEM((3, entries, patch), F32),
+            pltpu.SemaphoreType.DMA((2,)),
+            pltpu.SemaphoreType.DMA((tiles,)),
+        ],
+        compiler_params=pltpu.CompilerParams(vmem_limit_bytes=8 << 20),
+    )(fluid_tiles, weights, returned, pltpu.with_memory_space_constraint(owners, pltpu.HBM),
+      pltpu.with_memory_space_constraint(points_first, pltpu.HBM))
     return fluid, jnp.transpose(moved, (1, 0, 2))
 
 

time: 59 us -> 52 us (0.88)
  Pallas kernels: 58.2 us -> 51.2 us
    pallas_call x1, Pallas kernels: 54.9 us -> 46.9 us  [shards(): pl.pallas_call(functools.partial(step_kernel, rows_grid, columns_grid, pe...]
    pallas_call x1, Pallas kernels: 3.33 us -> 4.31 us  [shards(): pl.pallas_call(functools.partial(finish_kernel, devices, per_owner), out_...]
where the time goes in v1:
time: 52 us; the launch traced here: 51.8 us
  Pallas kernels  51.2 us (98%)
  between operations  0.64 us (1%)
    pallas_call x1, Pallas kernels, shards(): pl.pallas_call(functools.partial(step_kernel, rows_grid, columns_grid, pe...  46.9 us
    pallas_call x1, Pallas kernels, shards(): pl.pallas_call(functools.partial(finish_kernel, devices, per_owner), out_...  4.31 us

profile of v1, /device:TPU:0, one launch (start us, length us, event | category | flops | bytes accessed | tf_op | source)
XLA Modules:
  0.0 51.8 jit_solution(4421913424362249847)
XLA Ops:
  0.6 46.9 %shard_map.86 = (f32[4,3,32,32,128]{4,3,2,1,0:T(8,128)S(1)}, bf16[8,8,128,512]{3,2,1,0:T(8,128)(2,1)S(1)}, bf16[2,32,24,128]{3,2,1,0:T(8,128)(2,1)S(1)}) custom-call(f32[3,8,128]{2,1,0:T(8,128)} %bitcast.5, f32[8]{0:T(128)} %stiffness_in.1, s32[8,128]{1,0:T(8,128)} %links_in.1, s32[8,1,8]{2,1,0:T(1,128)} %bitcast.7, s32[8,8]{1,0:T(8,128)} %slots_in.1, ...), custom_call_target="tpu_custom_call" | custom-call | tf_op jit(solution)/shard_map/pallas_call | solution.py:568
  47.5 4.3 %shard_map.87 = (f32[3,32,32,512]{3,2,1,0:T(8,128)}, f32[3,8,128]{2,1,0:T(8,128)}) custom-call(f32[4,3,32,32,128]{4,3,2,1,0:T(8,128)S(1)} %get-tuple-element.7.fluid_ref, bf16[8,8,128,512]{3,2,1,0:T(8,128)(2,1)S(1)} %get-tuple-element.8.loaded_ref, bf16[2,32,24,128]{3,2,1,0:T(8,128)(2,1)S(1)} %get-tuple-element.9.returned_ref, s32[8,1,8]{2,1,0:T(1,128)} %bitcast.8, ...), custom_call_target="tpu_custom_call" | custom-call | tf_op jit(solution)/shard_map/pallas_call | solution.py:608

commit v2 on v1

--- a/solution.py
+++ b/solution.py
@@ -204,7 +204,7 @@
 def step_kernel(
     rows_grid, columns_grid, per_owner, points_in, stiffness_in, links_in, owners_in,
     slots_in, weights_ref, velocity_ref,
-    fluid_ref, loaded_ref, returned_ref,
+    fluid_ref, loaded_ref, returned_ref, partial_ref,
     points_ref, stiffness_ref, links_ref, owners_ref, slots_ref, small_sem, received_ref, table_ref, out_ref, outtable_ref, replies_ref, contrib_ref, stage_ref,
     force_ref, first_ref, second_ref, first_half, second_half, taking_ref, sides_send, sides_recv, ends_send, ends_recv,
     halo_ref, send_sem, recv_sem, load_sem, block_sem,
@@ -327,7 +327,13 @@
                 sends, receives))
         return out
 
-    def send_halo(step, ref, ends):
+    def send(step, wanted):
+        for copy, sends, _ in copies_of(step, wanted):
+            @pl.when(sends)
+            def _():
+                copy.start()
+
+    def send_sides(step, ref):
         flat = ref.reshape(flat_shape)
         for side in range(2):
             row = PAD + side * (rows - 1)
@@ -336,13 +342,13 @@
                     sides_send[step, side, c, t] = jnp.concatenate(
                         [flat[c, t, pl.ds(g * stride + row, 8, stride=stride), :]
                          for g in range(0, layers, 8)], axis=0).astype(BF16)
+        send(step, (0, 1))
+
+    def send_ends(step, ends):
         for side in range(2):
             for c in range(3):
                 ends_send[step, side, c] = ends[side * 3 + c]
-        for copy, sends, _ in copies_of(step):
-            @pl.when(sends)
-            def _():
-                copy.start()
+        send(step, (2, 3))
 
     def wait_ends(step):
         for copy, _, receives in copies_of(step, (2, 3)):
@@ -378,34 +384,43 @@
                 [ref[c, t, z, PAD + 8 * g + offset:PAD + 8 * g + offset + 8, :]
                  for g in pairs[k]], axis=0)
 
-        whole = [[beside(c, t, 0) for t in range(tiles)] for c in range(3)]
-        mids = [[v.astype(BF16) for v in row] for row in whole]
-        turned = {}
-
-        def turn(c, t, shift):
-            if (c, t, shift) not in turned:
-                if t < 0:
-                    v = pltpu.roll(halo_ref[0, c], lax.rem(LANES - j, LANES), 1)
-                elif t == tiles:
-                    v = pltpu.roll(halo_ref[1, c], LANES - 1 - j, 1)
-                else:
-                    v = pltpu.roll(mids[c][t], shift, 1)
-                turned[c, t, shift] = v
-            return turned[c, t, shift]
+        whole, mids = {}, {}
+
+        def mid(c, t):
+            if (c, t) not in mids:
+                whole[c, t] = beside(c, t, 0)
+                mids[c, t] = whole[c, t].astype(BF16)
+            return mids[c, t]
+
+        def north(c, t):
+            if t == tiles - 1:
+                after = pltpu.roll(halo_ref[1, c], lax.rem(LANES - j, LANES), 1)
+            else:
+                after = mid(c, t + 1)
+            return pltpu.roll(jnp.where(at_first, after, mid(c, t)), LANES - 1, 1)
+
+        def south(c, t):
+            if t == 0:
+                before = pltpu.roll(halo_ref[0, c], LANES - 1 - j, 1)
+            else:
+                before = mid(c, t - 1)
+            return pltpu.roll(jnp.where(at_last, before, mid(c, t)), 1, 1)
 
         for t in wanted:
             parts = []
             for c in range(3):
                 parts.append((
-                    mids[c][t], beside(c, t, 1).astype(BF16), beside(c, t, -1).astype(BF16),
-                    jnp.where(at_last, turn(c, t + 1, LANES - 1), turn(c, t, LANES - 1)),
-                    jnp.where(at_first, turn(c, t - 1, 1), turn(c, t, 1)),
+                    mid(c, t), beside(c, t, 1).astype(BF16), beside(c, t, -1).astype(BF16),
+                    north(c, t), south(c, t),
                     half[c, t, up, at, :], half[c, t, down, at, :]))
             change = sweep(*[list(v) for v in zip(*parts)])
-            yield t, [keep * whole[c][t] + transport_rate * change[c].astype(F32)
+            yield t, [keep * whole[c, t] + transport_rate * change[c].astype(F32)
                       for c in range(3)]
 
-    def run(ref, half, store, edge, groups_wanted, tiles_wanted, unroll, ends):
+    def run(ref, half, store, groups_wanted, tiles_wanted, ends=()):
+        edge = len(ends) > 0
+        unroll = max(1, min(layers, 4 * UNROLL // (len(groups_wanted) * len(tiles_wanted))))
+
         def body(i, ends):
             ends = list(ends)
             for m in range(unroll):
@@ -423,11 +438,12 @@
 
         return lax.fori_loop(0, layers // unroll, body, ends)
 
-    inner, outer = range(len(pairs) - 1), (len(pairs) - 1,)
-    every = range(tiles)
-    ends_zero = (zero,) * 6
+    inner, outer = tuple(range(len(pairs) - 1)), (len(pairs) - 1,)
+    middle, border = tuple(range(1, tiles - 1)), (0, tiles - 1)
+    half_tiles = tiles // 2
     ends = lax.fori_loop(0, layers // chunk, settle, (zero,) * 6)
-    send_halo(0, first_ref, ends)
+    send_ends(0, ends)
+    send_sides(0, first_ref)
     slots = table_column(table_ref, per_owner)
     taking_ref[...] = one_hot(iota((total, layers * rows), 1) == slots)
 
@@ -438,26 +454,31 @@
         second_half[c, t, z, 16 * k:16 * k + 16, :] = packed
         return packed
 
+    step_one = functools.partial(run, first_ref, first_half, store_first)
+    step_one(inner, middle)
     wait_ends(0)
-    ends = run(first_ref, first_half, store_first, True, inner, every, UNROLL, ends_zero)
     wait_sides(0, first_ref)
-    ends = run(first_ref, first_half, store_first, True, outer, every, UNROLL, ends)
-    send_halo(1, second_ref, ends)
+    ends = step_one(outer, border, (zero,) * 6)
+    step_one(outer, middle)
+    send_sides(1, second_ref)
+    ends = step_one(inner, border, ends)
+    send_ends(1, ends)
 
     def store_second(c, t, z, k, value):
         for m, g in enumerate(pairs[k]):
             fluid_ref[t, c, z, 8 * g:8 * g + 8, :] = value[8 * m:8 * m + 8]
 
-    half_tiles = tiles // 2
+    step_two = functools.partial(run, second_ref, second_half, store_second)
     wide = replies_ref.shape[2]
-    wait_ends(1)
     waits = []
+    step_two(inner, middle)
+    wait_sides(1, second_ref)
     for h in range(2):
         mine = range(h * half_tiles, (h + 1) * half_tiles)
-        run(second_ref, second_half, store_second, False, inner, mine, 2 * UNROLL, ())
+        step_two(outer, tuple(t for t in mine if t in middle))
         if h == 0:
-            wait_sides(1, second_ref)
-        run(second_ref, second_half, store_second, False, outer, mine, 2 * UNROLL, ())
+            wait_ends(1)
+        step_two(inner + outer, tuple(t for t in mine if t not in middle))
         for c in range(3):
             flat = jnp.concatenate(
                 [fluid_ref[t, c].reshape(layers * rows, LANES).astype(BF16) for t in mine], axis=1)
@@ -476,34 +497,38 @@
             @pl.when(sends)
             def _():
                 copy.wait_send()
-    for wait in waits:
-        wait()
-
-
-def interpolate(
-    devices, per_owner, returned_ref, loaded_ref, selector, stage_ref, picked_ref, points_ref, moved_ref,
-):
+    owner_row = to_row(owners_ref[:, 0, :])
+    places = slot_column(owner_row, to_column(owner_row), devices)
+    selector = one_hot(iota((places.shape[0], total), 1) == places)
+    waits[0]()
+
+    def emit(c, b, value):
+        partial_ref[c, b:b + 1, :] = value
+
+    interpolate(0, devices, per_owner, returned_ref, loaded_ref, selector, stage_ref, emit)
+    waits[1]()
+
+
+def interpolate(h, devices, per_owner, returned_ref, loaded_ref, selector, stage_ref, emit):
     blocks, k, points, patch = loaded_ref.shape
-    tiles = patch // LANES
-    half_tiles = tiles // 2
+    half_tiles = patch // LANES // 2
     wide = returned_ref.shape[2]
-    for h in range(2):
-        stage_ref[0:devices * wide, :] = returned_ref[h].astype(F32).reshape(
-            devices * wide, LANES)
-        for c in range(3):
-            replies = jnp.concatenate(
-                [jnp.concatenate(
-                    [stage_ref[pl.ds((p * 3 + c) * half_tiles + n, devices, stride=wide), :]
-                     for n in range(half_tiles)], axis=1)
-                 for p in range(per_owner)], axis=0).astype(BF16)
-            picked_ref[c, :, h * half_tiles * LANES:(h + 1) * half_tiles * LANES] = jnp.dot(
-                selector, replies, preferred_element_type=F32)
+    stage_ref[0:devices * wide, :] = returned_ref[h].astype(F32).reshape(devices * wide, LANES)
+    picked = []
+    for c in range(3):
+        replies = jnp.concatenate(
+            [jnp.concatenate(
+                [stage_ref[pl.ds((p * 3 + c) * half_tiles + n, devices, stride=wide), :]
+                 for n in range(half_tiles)], axis=1)
+             for p in range(per_owner)], axis=0).astype(BF16)
+        picked.append(jnp.dot(selector, replies, preferred_element_type=F32))
     diagonal = iota((k, k * points), 0) == iota((k, k * points), 1) // points
+    span = half_tiles * LANES
     for b in range(blocks):
-        rows = [picked_ref[c, b * k:(b + 1) * k, :] for c in range(3)]
+        rows = [picked[c][b * k:(b + 1) * k, :] for c in range(3)]
         rows.append(jnp.zeros_like(rows[0]))
         left = jnp.concatenate(rows, axis=0).astype(BF16)
-        right = loaded_ref[b].reshape(k * points, patch)
+        right = loaded_ref[b, :, :, h * span:(h + 1) * span].reshape(k * points, span)
         result = lax.dot_general(
             left, right, (((1,), (1,)), ((), ())), preferred_element_type=F32)
         for c in range(3):
@@ -511,13 +536,12 @@
             fold = own[:, 0:points]
             for n in range(1, k):
                 fold = fold + own[:, n * points:(n + 1) * points]
-            interp = jnp.sum(fold, axis=0, keepdims=True)
-            moved_ref[c, b:b + 1, :] = points_ref[c, b:b + 1, :] + fiber_step * interp
+            emit(c, b, jnp.sum(fold, axis=0, keepdims=True))
 
 
 def finish_kernel(
-    devices, per_owner, fluid_ref, loaded_ref, returned_ref, owners_in, points_in,
-    out_ref, moved_ref, owners_ref, points_ref, stage_ref, picked_ref, small_sem, store_sem,
+    devices, per_owner, fluid_ref, loaded_ref, returned_ref, partial_ref, owners_in, points_in,
+    out_ref, moved_ref, owners_ref, points_ref, stage_ref, small_sem, store_sem,
 ):
     def store(t):
         return pltpu.make_async_copy(
@@ -536,9 +560,12 @@
     owner_row = to_row(owners_ref[:, 0, :])
     places = slot_column(owner_row, to_column(owner_row), devices)
     selector = one_hot(iota((places.shape[0], devices * per_owner), 1) == places)
-    interpolate(
-        devices, per_owner, returned_ref, loaded_ref, selector, stage_ref, picked_ref, points_ref,
-        moved_ref)
+
+    def emit(c, b, value):
+        moved_ref[c, b:b + 1, :] = points_ref[c, b:b + 1, :] + fiber_step * (
+            partial_ref[c, b:b + 1, :] + value)
+
+    interpolate(1, devices, per_owner, returned_ref, loaded_ref, selector, stage_ref, emit)
     for t in range(fluid_ref.shape[0]):
         store(t).wait()
 
@@ -565,15 +592,16 @@
     half = pltpu.VMEM((3, tiles, layers, rows, LANES), BF16)
     sides = pltpu.VMEM((STEPS, 2, 3, tiles, layers, LANES), BF16)
     ends = pltpu.VMEM((STEPS, 2, 3, 16, LANES), BF16)
-    fluid_tiles, weights, returned = pl.pallas_call(
+    fluid_tiles, weights, returned, partial = pl.pallas_call(
         functools.partial(step_kernel, rows_grid, columns_grid, per_owner),
         out_shape=[
             jax.ShapeDtypeStruct((tiles, 3, layers, rows, LANES), F32),
             jax.ShapeDtypeStruct(delta_weights.shape, BF16),
             reply,
+            jax.ShapeDtypeStruct(points_first.shape, F32),
         ],
         in_specs=[HBM] * 7,
-        out_specs=[VMEM] * 3,
+        out_specs=[VMEM] * 4,
         scratch_shapes=[
             pltpu.VMEM(points_first.shape, F32),
             pltpu.SMEM(stiffness.shape, F32),
@@ -611,18 +639,17 @@
             jax.ShapeDtypeStruct(velocity.shape, F32),
             jax.ShapeDtypeStruct(points_first.shape, F32),
         ],
-        in_specs=[VMEM, VMEM, VMEM, HBM, HBM],
+        in_specs=[VMEM, VMEM, VMEM, VMEM, HBM, HBM],
         out_specs=[HBM, VMEM],
         scratch_shapes=[
             pltpu.VMEM(owners.shape, I32),
             pltpu.VMEM(points_first.shape, F32),
             stage,
-            pltpu.VMEM((3, entries, patch), F32),
             pltpu.SemaphoreType.DMA((2,)),
             pltpu.SemaphoreType.DMA((tiles,)),
         ],
         compiler_params=pltpu.CompilerParams(vmem_limit_bytes=8 << 20),
-    )(fluid_tiles, weights, returned, pltpu.with_memory_space_constraint(owners, pltpu.HBM),
+    )(fluid_tiles, weights, returned, partial, pltpu.with_memory_space_constraint(owners, pltpu.HBM),
       pltpu.with_memory_space_constraint(points_first, pltpu.HBM))
     return fluid, jnp.transpose(moved, (1, 0, 2))
 

time: 52 us -> 49.6 us (0.954)
  Pallas kernels: 51.2 us -> 48.7 us
    pallas_call x1, Pallas kernels: 46.9 us -> 45.4 us  [shards(): pl.pallas_call(functools.partial(step_kernel, rows_grid, columns_grid, pe...]
    pallas_call x1, Pallas kernels: 4.31 us -> 3.35 us  [shards(): pl.pallas_call(functools.partial(finish_kernel, devices, per_owner), out_...]
where the time goes in v2:
time: 49.6 us; the launch traced here: 49.4 us
  Pallas kernels  48.7 us (98%)
  between operations  0.64 us (1%)
    pallas_call x1, Pallas kernels, shards(): pl.pallas_call(functools.partial(step_kernel, rows_grid, columns_grid, pe...  45.4 us
    pallas_call x1, Pallas kernels, shards(): pl.pallas_call(functools.partial(finish_kernel, devices, per_owner), out_...  3.35 us

profile of v2, /device:TPU:0, one launch (start us, length us, event | category | flops | bytes accessed | tf_op | source)
XLA Modules:
  0.0 49.4 jit_solution(17677983343996348327)
XLA Ops:
  0.6 45.4 %shard_map.86 = (f32[4,3,32,32,128]{4,3,2,1,0:T(8,128)S(1)}, bf16[8,8,128,512]{3,2,1,0:T(8,128)(2,1)S(1)}, bf16[2,32,24,128]{3,2,1,0:T(8,128)(2,1)S(1)}, f32[3,8,128]{2,1,0:T(8,128)S(1)}) custom-call(f32[3,8,128]{2,1,0:T(8,128)} %bitcast.5, f32[8]{0:T(128)} %stiffness_in.1, s32[8,128]{1,0:T(8,128)} %links_in.1, s32[8,1,8]{2,1,0:T(1,128)} %bitcast.7, ...), custom_call_target="tpu_custom_call" | custom-call | tf_op jit(solution)/shard_map/pallas_call | solution.py:595
  46.0 3.4 %shard_map.87 = (f32[3,32,32,512]{3,2,1,0:T(8,128)}, f32[3,8,128]{2,1,0:T(8,128)}) custom-call(f32[4,3,32,32,128]{4,3,2,1,0:T(8,128)S(1)} %get-tuple-element.8.fluid_ref, bf16[8,8,128,512]{3,2,1,0:T(8,128)(2,1)S(1)} %get-tuple-element.9.loaded_ref, bf16[2,32,24,128]{3,2,1,0:T(8,128)(2,1)S(1)} %get-tuple-element.10.returned_ref, ...), custom_call_target="tpu_custom_call" | custom-call | tf_op jit(solution)/shard_map/pallas_call | solution.py:636

commit v3 on v2

--- a/solution.py
+++ b/solution.py
@@ -275,21 +275,28 @@
     lane = iota((16, LANES), 1)
     at_first, at_last = lane == 0, lane == LANES - 1
 
-    unit = one_hot(at_first)
-
-    def gather_end(side, mark, j, value, total_so_far):
-        shift = j if side == 0 else lax.rem(j + 1, LANES)
-        return total_so_far + mark * pltpu.roll(value, shift, 1)
+    unit = one_hot(at_first | at_last)
+
+    def edge_lane(z, k):
+        return 2 * (z * len(pairs) + k) + 1
+
+    def gather_end(j, mark, low, high, total_so_far):
+        return total_so_far + mark * pltpu.roll(jnp.where(at_first, low, high), j, 1)
 
     zero = jnp.zeros((16, LANES), BF16)
 
     def settle(n, ends):
         ends = list(ends)
         placing = one_hot(iota((cells, total), 0) + n * cells == slots_row)
+        marks = {
+            (k, n_pair): pltpu.roll(unit, edge_lane(n * chunk + k, n_pair), 1)
+            for k in range(chunk) for n_pair in range(len(pairs))
+        }
         for c in range(3):
             push = jnp.dot(placing, force_ref[c], preferred_element_type=F32)
             for k in range(chunk):
                 z = n * chunk + k
+                edges = {}
                 for t in range(tiles):
                     value = fluid_ref[t, c, z] + push[
                         k * rows:(k + 1) * rows, t * LANES:(t + 1) * LANES]
@@ -298,12 +305,11 @@
                         packed = jnp.concatenate(
                             [value[8 * g:8 * g + 8] for g in pair], axis=0).astype(BF16)
                         first_half[c, t, z, 16 * n_pair:16 * n_pair + 16, :] = packed
-                        for side in range(2):
-                            if t == side * (tiles - 1):
-                                n_end = side * 3 + c
-                                j = z * len(pairs) + n_pair
-                                ends[n_end] = gather_end(
-                                    side, pltpu.roll(unit, j, 1), j, packed, ends[n_end])
+                        edges[t, n_pair] = packed
+                for n_pair in range(len(pairs)):
+                    ends[c] = gather_end(
+                        edge_lane(z, n_pair), marks[k, n_pair], edges[0, n_pair],
+                        edges[tiles - 1, n_pair], ends[c])
         return tuple(ends)
 
     has = [gx > 0, gx < rows_grid - 1, gy > 0, gy < columns_grid - 1]
@@ -312,8 +318,8 @@
         plan = [
             (sides_send.at[step, 0], sides_recv.at[step, 1], (-1, 0), has[0], has[1]),
             (sides_send.at[step, 1], sides_recv.at[step, 0], (1, 0), has[1], has[0]),
-            (ends_send.at[step, 0], ends_recv.at[step, 1], (0, -1), has[2], has[3]),
-            (ends_send.at[step, 1], ends_recv.at[step, 0], (0, 1), has[3], has[2]),
+            (ends_send.at[step], ends_recv.at[step, 1], (0, -1), has[2], has[3]),
+            (ends_send.at[step], ends_recv.at[step, 0], (0, 1), has[3], has[2]),
         ]
         out = []
         for n, (source, target, (dx, dy), sends, receives) in enumerate(plan):
@@ -345,9 +351,8 @@
         send(step, (0, 1))
 
     def send_ends(step, ends):
-        for side in range(2):
-            for c in range(3):
-                ends_send[step, side, c] = ends[side * 3 + c]
+        for c in range(3):
+            ends_send[step, c] = ends[c]
         send(step, (2, 3))
 
     def wait_ends(step):
@@ -355,10 +360,11 @@
             @pl.when(receives)
             def _():
                 copy.wait_recv()
-        for side in range(2):
-            for c in range(3):
-                halo_ref[side, c] = jnp.where(
-                    has[2 + side], ends_recv[step, side, c].astype(F32), 0.0).astype(BF16)
+        even = lax.rem(lane, 2) == 0
+        for c in range(3):
+            south, north = [ends_recv[step, side, c].astype(F32) for side in range(2)]
+            halo_ref[c] = jnp.where(
+                even, jnp.where(has[2], south, 0.0), jnp.where(has[3], north, 0.0)).astype(BF16)
 
     def wait_sides(step, ref):
         flat = ref.reshape(flat_shape)
@@ -376,7 +382,7 @@
 
     def sweep_tiles(ref, half, z, k, wanted):
         up, down = lax.rem(z + 1, layers), lax.rem(z + layers - 1, layers)
-        j = z * len(pairs) + k
+        j = edge_lane(z, k)
         at = slice(16 * k, 16 * k + 16)
 
         def beside(c, t, offset):
@@ -392,16 +398,23 @@
                 mids[c, t] = whole[c, t].astype(BF16)
             return mids[c, t]
 
+        outside = {}
+
+        def beyond(c):
+            if c not in outside:
+                outside[c] = pltpu.roll(halo_ref[c], LANES - j, 1)
+            return outside[c]
+
         def north(c, t):
             if t == tiles - 1:
-                after = pltpu.roll(halo_ref[1, c], lax.rem(LANES - j, LANES), 1)
+                after = beyond(c)
             else:
                 after = mid(c, t + 1)
             return pltpu.roll(jnp.where(at_first, after, mid(c, t)), LANES - 1, 1)
 
         def south(c, t):
             if t == 0:
-                before = pltpu.roll(halo_ref[0, c], LANES - 1 - j, 1)
+                before = beyond(c)
             else:
                 before = mid(c, t - 1)
             return pltpu.roll(jnp.where(at_last, before, mid(c, t)), 1, 1)
@@ -426,14 +439,16 @@
             for m in range(unroll):
                 z = i * unroll + m
                 for k in groups_wanted:
-                    j = z * len(pairs) + k
-                    mark = pltpu.roll(unit, j, 1)
+                    edges = {}
                     for t, new in sweep_tiles(ref, half, z, k, tiles_wanted):
                         for c in range(3):
-                            packed = store(c, t, z, k, new[c])
-                            if edge and t in (0, tiles - 1):
-                                n_end = (0 if t == 0 else 3) + c
-                                ends[n_end] = gather_end(t > 0, mark, j, packed, ends[n_end])
+                            edges[c, t] = store(c, t, z, k, new[c])
+                    if edge:
+                        j = edge_lane(z, k)
+                        mark = pltpu.roll(unit, j, 1)
+                        for c in range(3):
+                            ends[c] = gather_end(
+                                j, mark, edges[c, 0], edges[c, tiles - 1], ends[c])
             return tuple(ends)
 
         return lax.fori_loop(0, layers // unroll, body, ends)
@@ -441,7 +456,7 @@
     inner, outer = tuple(range(len(pairs) - 1)), (len(pairs) - 1,)
     middle, border = tuple(range(1, tiles - 1)), (0, tiles - 1)
     half_tiles = tiles // 2
-    ends = lax.fori_loop(0, layers // chunk, settle, (zero,) * 6)
+    ends = lax.fori_loop(0, layers // chunk, settle, (zero,) * 3)
     send_ends(0, ends)
     send_sides(0, first_ref)
     slots = table_column(table_ref, per_owner)
@@ -457,12 +472,12 @@
     step_one = functools.partial(run, first_ref, first_half, store_first)
     step_one(inner, middle)
     wait_ends(0)
+    ends = step_one(inner, border, (zero,) * 3)
     wait_sides(0, first_ref)
-    ends = step_one(outer, border, (zero,) * 6)
+    ends = step_one(outer, border, ends)
+    send_ends(1, ends)
     step_one(outer, middle)
     send_sides(1, second_ref)
-    ends = step_one(inner, border, ends)
-    send_ends(1, ends)
 
     def store_second(c, t, z, k, value):
         for m, g in enumerate(pairs[k]):
@@ -472,13 +487,12 @@
     wide = replies_ref.shape[2]
     waits = []
     step_two(inner, middle)
+    wait_ends(1)
+    step_two(inner, border)
     wait_sides(1, second_ref)
     for h in range(2):
-        mine = range(h * half_tiles, (h + 1) * half_tiles)
-        step_two(outer, tuple(t for t in mine if t in middle))
-        if h == 0:
-            wait_ends(1)
-        step_two(inner + outer, tuple(t for t in mine if t not in middle))
+        mine = tuple(range(h * half_tiles, (h + 1) * half_tiles))
+        step_two(outer, mine)
         for c in range(3):
             flat = jnp.concatenate(
                 [fluid_ref[t, c].reshape(layers * rows, LANES).astype(BF16) for t in mine], axis=1)
@@ -591,7 +605,6 @@
     field = pltpu.VMEM((3, tiles, layers, rows + 2 * PAD, LANES), F32)
     half = pltpu.VMEM((3, tiles, layers, rows, LANES), BF16)
     sides = pltpu.VMEM((STEPS, 2, 3, tiles, layers, LANES), BF16)
-    ends = pltpu.VMEM((STEPS, 2, 3, 16, LANES), BF16)
     fluid_tiles, weights, returned, partial = pl.pallas_call(
         functools.partial(step_kernel, rows_grid, columns_grid, per_owner),
         out_shape=[
@@ -619,8 +632,10 @@
             pltpu.VMEM((3, total, patch), BF16),
             field, field, half, half,
             pltpu.VMEM((total, layers * rows), BF16),
-            sides, sides, ends, ends,
-            pltpu.VMEM((2, 3, 16, LANES), BF16),
+            sides, sides,
+            pltpu.VMEM((STEPS, 3, 16, LANES), BF16),
+            pltpu.VMEM((STEPS, 2, 3, 16, LANES), BF16),
+            pltpu.VMEM((3, 16, LANES), BF16),
             pltpu.SemaphoreType.DMA((4,)),
             pltpu.SemaphoreType.DMA((4,)),
             pltpu.SemaphoreType.DMA((tiles,)),

time: 49.6 us -> 48.8 us (0.984)
  Pallas kernels: 48.7 us -> 48 us
    pallas_call x1, Pallas kernels: 45.4 us -> 44.6 us  [shards(): pl.pallas_call(functools.partial(step_kernel, rows_grid, columns_grid, pe...]
where the time goes in v3:
time: 48.8 us; the launch traced here: 48.6 us
  Pallas kernels  48 us (98%)
  between operations  0.64 us (1%)
    pallas_call x1, Pallas kernels, shards(): pl.pallas_call(functools.partial(step_kernel, rows_grid, columns_grid, pe...  44.6 us
    pallas_call x1, Pallas kernels, shards(): pl.pallas_call(functools.partial(finish_kernel, devices, per_owner), out_...  3.35 us

profile of v3, /device:TPU:0, one launch (start us, length us, event | category | flops | bytes accessed | tf_op | source)
XLA Modules:
  0.0 48.6 jit_solution(4873333931947492927)
XLA Ops:
  0.6 44.6 %shard_map.86 = (f32[4,3,32,32,128]{4,3,2,1,0:T(8,128)S(1)}, bf16[8,8,128,512]{3,2,1,0:T(8,128)(2,1)S(1)}, bf16[2,32,24,128]{3,2,1,0:T(8,128)(2,1)S(1)}, f32[3,8,128]{2,1,0:T(8,128)S(1)}) custom-call(f32[3,8,128]{2,1,0:T(8,128)} %bitcast.5, f32[8]{0:T(128)} %stiffness_in.1, s32[8,128]{1,0:T(8,128)} %links_in.1, s32[8,1,8]{2,1,0:T(1,128)} %bitcast.7, ...), custom_call_target="tpu_custom_call" | custom-call | tf_op jit(solution)/shard_map/pallas_call | solution.py:608
  45.2 3.4 %shard_map.87 = (f32[3,32,32,512]{3,2,1,0:T(8,128)}, f32[3,8,128]{2,1,0:T(8,128)}) custom-call(f32[4,3,32,32,128]{4,3,2,1,0:T(8,128)S(1)} %get-tuple-element.8.fluid_ref, bf16[8,8,128,512]{3,2,1,0:T(8,128)(2,1)S(1)} %get-tuple-element.9.loaded_ref, bf16[2,32,24,128]{3,2,1,0:T(8,128)(2,1)S(1)} %get-tuple-element.10.returned_ref, ...), custom_call_target="tpu_custom_call" | custom-call | tf_op jit(solution)/shard_map/pallas_call | solution.py:651

commit v4 on v3

--- a/solution.py
+++ b/solution.py
@@ -206,7 +206,7 @@
     slots_in, weights_ref, velocity_ref,
     fluid_ref, loaded_ref, returned_ref, partial_ref,
     points_ref, stiffness_ref, links_ref, owners_ref, slots_ref, small_sem, received_ref, table_ref, out_ref, outtable_ref, replies_ref, contrib_ref, stage_ref,
-    force_ref, first_ref, second_ref, first_half, second_half, taking_ref, sides_send, sides_recv, ends_send, ends_recv,
+    force_ref, first_ref, second_ref, first_half, second_half, placing_ref, taking_ref, sides_send, sides_recv, ends_send, ends_recv,
     halo_ref, send_sem, recv_sem, load_sem, block_sem,
     hsend_sem, hrecv_sem,
 ):
@@ -264,14 +264,19 @@
     for t in range(tiles):
         load(t).wait()
     wait_table()
+    chunk = 8
+    cells = chunk * rows
+    slots_row = table_row(table_ref, devices, per_owner)
+    placing_ref[...] = one_hot(iota((layers * rows, total), 0) == slots_row)
+    slots = table_column(table_ref, per_owner)
+    taking_ref[...] = one_hot(iota((total, layers * rows), 1) == slots)
     wait()
 
     stage_ref[...] = received_ref[...].astype(F32).reshape(stage_ref.shape)
     for c in range(3):
-        force_ref[c] = (force_step * unpack(stage_ref, devices, per_owner, tiles, c)).astype(BF16)
-    slots_row = table_row(table_ref, devices, per_owner)
-    chunk = 8
-    cells = chunk * rows
+        force = (force_step * unpack(stage_ref, devices, per_owner, tiles, c)).astype(BF16)
+        for n, t in enumerate((0, tiles - 1, *range(1, tiles - 1))):
+            force_ref[c, :, n * LANES:(n + 1) * LANES] = force[:, t * LANES:(t + 1) * LANES]
     lane = iota((16, LANES), 1)
     at_first, at_last = lane == 0, lane == LANES - 1
 
@@ -285,28 +290,30 @@
 
     zero = jnp.zeros((16, LANES), BF16)
 
-    def settle(n, ends):
+    def settle(first, wanted, n, ends):
         ends = list(ends)
-        placing = one_hot(iota((cells, total), 0) + n * cells == slots_row)
+        placing = placing_ref[pl.ds(pl.multiple_of(n * cells, cells), cells), :]
         marks = {
             (k, n_pair): pltpu.roll(unit, edge_lane(n * chunk + k, n_pair), 1)
-            for k in range(chunk) for n_pair in range(len(pairs))
+            for k in range(chunk) for n_pair in range(len(pairs)) if ends
         }
         for c in range(3):
-            push = jnp.dot(placing, force_ref[c], preferred_element_type=F32)
+            push = jnp.dot(
+                placing, force_ref[c, :, first * LANES:(first + len(wanted)) * LANES],
+                preferred_element_type=F32)
             for k in range(chunk):
                 z = n * chunk + k
                 edges = {}
-                for t in range(tiles):
+                for m, t in enumerate(wanted):
                     value = fluid_ref[t, c, z] + push[
-                        k * rows:(k + 1) * rows, t * LANES:(t + 1) * LANES]
+                        k * rows:(k + 1) * rows, m * LANES:(m + 1) * LANES]
                     first_ref[c, t, z, PAD:PAD + rows, :] = value
                     for n_pair, pair in enumerate(pairs):
                         packed = jnp.concatenate(
                             [value[8 * g:8 * g + 8] for g in pair], axis=0).astype(BF16)
                         first_half[c, t, z, 16 * n_pair:16 * n_pair + 16, :] = packed
                         edges[t, n_pair] = packed
-                for n_pair in range(len(pairs)):
+                for n_pair in range(len(pairs) if ends else 0):
                     ends[c] = gather_end(
                         edge_lane(z, n_pair), marks[k, n_pair], edges[0, n_pair],
                         edges[tiles - 1, n_pair], ends[c])
@@ -456,12 +463,11 @@
     inner, outer = tuple(range(len(pairs) - 1)), (len(pairs) - 1,)
     middle, border = tuple(range(1, tiles - 1)), (0, tiles - 1)
     half_tiles = tiles // 2
-    ends = lax.fori_loop(0, layers // chunk, settle, (zero,) * 3)
+    ends = lax.fori_loop(
+        0, layers // chunk, functools.partial(settle, 0, border), (zero,) * 3)
     send_ends(0, ends)
+    lax.fori_loop(0, layers // chunk, functools.partial(settle, len(border), middle), ())
     send_sides(0, first_ref)
-    slots = table_column(table_ref, per_owner)
-    taking_ref[...] = one_hot(iota((total, layers * rows), 1) == slots)
-
     def store_first(c, t, z, k, value):
         for m, g in enumerate(pairs[k]):
             second_ref[c, t, z, PAD + 8 * g:PAD + 8 * g + 8, :] = value[8 * m:8 * m + 8]
@@ -601,7 +607,7 @@
     reply = jax.ShapeDtypeStruct((2, devices, wide, LANES), BF16)
     table_shape = jax.ShapeDtypeStruct((devices, 1, LANES), I32)
     stage = pltpu.VMEM((devices * max(width, wide), LANES), F32)
-    limit = 32 << 20
+    limit = 36 << 20
     field = pltpu.VMEM((3, tiles, layers, rows + 2 * PAD, LANES), F32)
     half = pltpu.VMEM((3, tiles, layers, rows, LANES), BF16)
     sides = pltpu.VMEM((STEPS, 2, 3, tiles, layers, LANES), BF16)
@@ -631,6 +637,7 @@
             stage,
             pltpu.VMEM((3, total, patch), BF16),
             field, field, half, half,
+            pltpu.VMEM((layers * rows, total), BF16),
             pltpu.VMEM((total, layers * rows), BF16),
             sides, sides,
             pltpu.VMEM((STEPS, 3, 16, LANES), BF16),

time: 48.8 us -> 48.4 us (level)
  no operation moved by 1% of the time
where the time goes in v4:
time: 48.4 us; the launch traced here: 48.2 us
  Pallas kernels  47.6 us (98%)
  between operations  0.64 us (1%)
    pallas_call x1, Pallas kernels, shards(): pl.pallas_call(functools.partial(step_kernel, rows_grid, columns_grid, pe...  44.2 us
    pallas_call x1, Pallas kernels, shards(): pl.pallas_call(functools.partial(finish_kernel, devices, per_owner), out_...  3.35 us

profile of v4, /device:TPU:0, one launch (start us, length us, event | category | flops | bytes accessed | tf_op | source)
XLA Modules:
  0.0 48.2 jit_solution(8463752593586753254)
XLA Ops:
  0.6 44.2 %shard_map.86 = (f32[4,3,32,32,128]{4,3,2,1,0:T(8,128)S(1)}, bf16[8,8,128,512]{3,2,1,0:T(8,128)(2,1)S(1)}, bf16[2,32,24,128]{3,2,1,0:T(8,128)(2,1)S(1)}, f32[3,8,128]{2,1,0:T(8,128)S(1)}) custom-call(f32[3,8,128]{2,1,0:T(8,128)} %bitcast.5, f32[8]{0:T(128)} %stiffness_in.1, s32[8,128]{1,0:T(8,128)} %links_in.1, s32[8,1,8]{2,1,0:T(1,128)} %bitcast.7, ...), custom_call_target="tpu_custom_call" | custom-call | tf_op jit(solution)/shard_map/pallas_call | solution.py:614
  44.9 3.4 %shard_map.87 = (f32[3,32,32,512]{3,2,1,0:T(8,128)}, f32[3,8,128]{2,1,0:T(8,128)}) custom-call(f32[4,3,32,32,128]{4,3,2,1,0:T(8,128)S(1)} %get-tuple-element.8.fluid_ref, bf16[8,8,128,512]{3,2,1,0:T(8,128)(2,1)S(1)} %get-tuple-element.9.loaded_ref, bf16[2,32,24,128]{3,2,1,0:T(8,128)(2,1)S(1)} %get-tuple-element.10.returned_ref, ...), custom_call_target="tpu_custom_call" | custom-call | tf_op jit(solution)/shard_map/pallas_call | solution.py:658

commit v5 on v4

--- a/solution.py
+++ b/solution.py
@@ -321,10 +321,12 @@
 
     has = [gx > 0, gx < rows_grid - 1, gy > 0, gy < columns_grid - 1]
 
-    def copies_of(step, wanted=range(4)):
+    def copies_of(step, wanted=range(6)):
         plan = [
-            (sides_send.at[step, 0], sides_recv.at[step, 1], (-1, 0), has[0], has[1]),
-            (sides_send.at[step, 1], sides_recv.at[step, 0], (1, 0), has[1], has[0]),
+            *[(sides_send.at[step, part, 0], sides_recv.at[step, part, 1], (-1, 0), has[0], has[1])
+              for part in range(2)],
+            *[(sides_send.at[step, part, 1], sides_recv.at[step, part, 0], (1, 0), has[1], has[0])
+              for part in range(2)],
             (ends_send.at[step], ends_recv.at[step, 1], (0, -1), has[2], has[3]),
             (ends_send.at[step], ends_recv.at[step, 0], (0, 1), has[3], has[2]),
         ]
@@ -346,24 +348,24 @@
             def _():
                 copy.start()
 
-    def send_sides(step, ref):
+    def send_sides(step, ref, part):
         flat = ref.reshape(flat_shape)
         for side in range(2):
             row = PAD + side * (rows - 1)
             for c in range(3):
-                for t in range(tiles):
-                    sides_send[step, side, c, t] = jnp.concatenate(
+                for n, t in enumerate((border, middle)[part]):
+                    sides_send[step, part, side, c, n] = jnp.concatenate(
                         [flat[c, t, pl.ds(g * stride + row, 8, stride=stride), :]
                          for g in range(0, layers, 8)], axis=0).astype(BF16)
-        send(step, (0, 1))
+        send(step, (part, 2 + part))
 
     def send_ends(step, ends):
         for c in range(3):
             ends_send[step, c] = ends[c]
-        send(step, (2, 3))
+        send(step, (4, 5))
 
     def wait_ends(step):
-        for copy, _, receives in copies_of(step, (2, 3)):
+        for copy, _, receives in copies_of(step, (4, 5)):
             @pl.when(receives)
             def _():
                 copy.wait_recv()
@@ -375,17 +377,20 @@
 
     def wait_sides(step, ref):
         flat = ref.reshape(flat_shape)
-        for copy, _, receives in copies_of(step, (0, 1)):
+        for copy, _, receives in copies_of(step, range(4)):
             @pl.when(receives)
             def _():
                 copy.wait_recv()
         for side in range(2):
             row = PAD - 1 if side == 0 else PAD + rows
-            for c in range(3):
-                for t in range(tiles):
-                    value = jnp.where(has[side], sides_recv[step, side, c, t].astype(F32), 0.0)
-                    for g in range(0, layers, 8):
-                        flat[c, t, pl.ds(g * stride + row, 8, stride=stride), :] = value[g:g + 8]
+            for part in range(2):
+                for c in range(3):
+                    for n, t in enumerate((border, middle)[part]):
+                        value = jnp.where(
+                            has[side], sides_recv[step, part, side, c, n].astype(F32), 0.0)
+                        for g in range(0, layers, 8):
+                            flat[c, t, pl.ds(g * stride + row, 8, stride=stride), :] = (
+                                value[g:g + 8])
 
     def sweep_tiles(ref, half, z, k, wanted):
         up, down = lax.rem(z + 1, layers), lax.rem(z + layers - 1, layers)
@@ -466,8 +471,9 @@
     ends = lax.fori_loop(
         0, layers // chunk, functools.partial(settle, 0, border), (zero,) * 3)
     send_ends(0, ends)
+    send_sides(0, first_ref, 0)
     lax.fori_loop(0, layers // chunk, functools.partial(settle, len(border), middle), ())
-    send_sides(0, first_ref)
+    send_sides(0, first_ref, 1)
     def store_first(c, t, z, k, value):
         for m, g in enumerate(pairs[k]):
             second_ref[c, t, z, PAD + 8 * g:PAD + 8 * g + 8, :] = value[8 * m:8 * m + 8]
@@ -482,8 +488,9 @@
     wait_sides(0, first_ref)
     ends = step_one(outer, border, ends)
     send_ends(1, ends)
+    send_sides(1, second_ref, 0)
     step_one(outer, middle)
-    send_sides(1, second_ref)
+    send_sides(1, second_ref, 1)
 
     def store_second(c, t, z, k, value):
         for m, g in enumerate(pairs[k]):
@@ -610,7 +617,7 @@
     limit = 36 << 20
     field = pltpu.VMEM((3, tiles, layers, rows + 2 * PAD, LANES), F32)
     half = pltpu.VMEM((3, tiles, layers, rows, LANES), BF16)
-    sides = pltpu.VMEM((STEPS, 2, 3, tiles, layers, LANES), BF16)
+    sides = pltpu.VMEM((STEPS, 2, 2, 3, tiles // 2, layers, LANES), BF16)
     fluid_tiles, weights, returned, partial = pl.pallas_call(
         functools.partial(step_kernel, rows_grid, columns_grid, per_owner),
         out_shape=[
@@ -647,8 +654,8 @@
             pltpu.SemaphoreType.DMA((4,)),
             pltpu.SemaphoreType.DMA((tiles,)),
             pltpu.SemaphoreType.DMA((blocks,)),
-            pltpu.SemaphoreType.DMA((STEPS, 4)),
-            pltpu.SemaphoreType.DMA((STEPS, 4)),
+            pltpu.SemaphoreType.DMA((STEPS, 6)),
+            pltpu.SemaphoreType.DMA((STEPS, 6)),
         ],
         compiler_params=pltpu.CompilerParams(
             collective_id=0, has_side_effects=True, vmem_limit_bytes=limit),

time: 48.4 us -> 48.2 us (level)
  no operation moved by 1% of the time
where the time goes in v5:
time: 48.2 us; the launch traced here: 48 us
  Pallas kernels  47.4 us (98%)
  between operations  0.64 us (1%)
    pallas_call x1, Pallas kernels, shards(): pl.pallas_call(functools.partial(step_kernel, rows_grid, columns_grid, pe...  44 us
    pallas_call x1, Pallas kernels, shards(): pl.pallas_call(functools.partial(finish_kernel, devices, per_owner), out_...  3.35 us

profile of v5, /device:TPU:0, one launch (start us, length us, event | category | flops | bytes accessed | tf_op | source)
XLA Modules:
  0.0 48.0 jit_solution(1087443641833493728)
XLA Ops:
  0.6 44.0 %shard_map.86 = (f32[4,3,32,32,128]{4,3,2,1,0:T(8,128)S(1)}, bf16[8,8,128,512]{3,2,1,0:T(8,128)(2,1)S(1)}, bf16[2,32,24,128]{3,2,1,0:T(8,128)(2,1)S(1)}, f32[3,8,128]{2,1,0:T(8,128)S(1)}) custom-call(f32[3,8,128]{2,1,0:T(8,128)} %bitcast.5, f32[8]{0:T(128)} %stiffness_in.1, s32[8,128]{1,0:T(8,128)} %links_in.1, s32[8,1,8]{2,1,0:T(1,128)} %bitcast.7, ...), custom_call_target="tpu_custom_call" | custom-call | tf_op jit(solution)/shard_map/pallas_call | solution.py:621
  44.7 3.4 %shard_map.87 = (f32[3,32,32,512]{3,2,1,0:T(8,128)}, f32[3,8,128]{2,1,0:T(8,128)}) custom-call(f32[4,3,32,32,128]{4,3,2,1,0:T(8,128)S(1)} %get-tuple-element.8.fluid_ref, bf16[8,8,128,512]{3,2,1,0:T(8,128)(2,1)S(1)} %get-tuple-element.9.loaded_ref, bf16[2,32,24,128]{3,2,1,0:T(8,128)(2,1)S(1)} %get-tuple-element.10.returned_ref, ...), custom_call_target="tpu_custom_call" | custom-call | tf_op jit(solution)/shard_map/pallas_call | solution.py:665
